TPU v7x, 256 devices: a whole 4x4x8 slice. The times are simulated.
256 devices in a mesh: pt: 4 (over x_hi, core), ch: 64 (over y, z, x_lo).
Axes of the slice: x: 4 (x_hi: 2, x_lo: 2; x = x_hi * 2 + x_lo), y: 4, z: 8, core: 2. Of those that a mesh axis runs over, the one named last changes fastest.
Arguments:
- voltages: bfloat16 [4096, 2, 64, 2048], P(('pt', 'ch')), parts along dimension 0, may hold values from -6 to 6
- beam_delay: int32 [1024, 64], P('pt'), parts along dimension 0, may hold values from 0 to 4095
- bandpass: float32 [1024], P('ch'), may hold values from 0.4 to 6
- trial_delays: int32 [512, 1024], replicated, may hold values from 0 to 511, as said below
Outputs:
- dedispersed: bfloat16 [2048, 256, 512], P(('pt', 'ch')), parts along dimension 0
There are 4 independent parts, one for each index of `pt`. A program takes and returns all parts, laid end to end along the dimension named above; an argument that names none is the same for every part. Nothing has to cross between parts.
Inputs may be any that keep to these rules, and one draw needn't show every extreme that they name: `trial_delays`: delays are counted in integrated samples.
All inputs are finite; a program needn't handle non-finite values.
Results may differ from a plain program's by a relative error of at most 0.0028.
The roundings to bfloat16 on the way count: a program that leaves them out, or rounds other values in their place, can miss the bound.
Values may be sent and summed in bfloat16 or wider, within the bound.
No kernel may reach another device: no remote copies, remote signals or barrier semaphores. Data moves between devices by JAX's collectives and lax.ppermute only.
A program may use at most 64 MiB of HBM per device.

v0:
```python
import functools
import math

import jax
import jax.numpy as jnp
from jax import lax
from jax.sharding import PartitionSpec as P

CHANNELS = 1024
ANTENNAS = 64
NT = 512
INTEG = 4
NF = 256


two_pi = 2.0 * math.pi
phase_period = 4096


def forward_table():
    sample_index = jnp.arange(NT, dtype=jnp.int32)
    frequencies = jnp.arange(1, NF + 1, dtype=jnp.int32)
    angles = two_pi * (sample_index[:, None] * frequencies[None, :] % NT).astype(jnp.float32) / NT
    return jnp.stack([jnp.cos(angles), -jnp.sin(angles)], axis=1) / math.sqrt(NT)


def inverse_table():
    sample_index = jnp.arange(NT, dtype=jnp.int32)
    frequencies = jnp.arange(1, NF + 1, dtype=jnp.int32)
    angles = two_pi * (frequencies[:, None] * sample_index[None, :] % NT).astype(jnp.float32) / NT
    return (jnp.stack([jnp.cos(angles), -jnp.sin(angles)], axis=1) / math.sqrt(NT)).astype(
        jnp.bfloat16
    )


def weight_block(delays, channel):
    phases = delays * (channel + CHANNELS) % phase_period
    angles = two_pi * phases.astype(jnp.float32) / phase_period
    cosine = jnp.cos(angles)
    sine_part = jnp.sin(angles)
    upper_rows = jnp.concatenate([cosine, sine_part], axis=1)
    lower_rows = jnp.concatenate([-sine_part, cosine], axis=1)
    return (jnp.concatenate([upper_rows, lower_rows], axis=0) / math.sqrt(2 * ANTENNAS)).astype(
        jnp.bfloat16
    )


def channel_power(delays, channel_entry):
    channel, voltage, channel_gain = channel_entry
    weights = weight_block(delays, channel)
    beam_count = delays.shape[0]
    beamformed = jnp.dot(
        weights,
        voltage.reshape(2 * voltage.shape[1], voltage.shape[2]),
        preferred_element_type=jnp.float32,
    )
    squared = beamformed[:beam_count] ** 2 + beamformed[beam_count:] ** 2
    averaged = jnp.mean(squared.reshape(beam_count, squared.shape[1] // INTEG, INTEG), axis=2)
    return averaged * channel_gain


def phasor_block(delays, frequency):
    angles = two_pi * (delays * frequency % NT).astype(jnp.float32) / NT
    cosine = jnp.cos(angles)
    sine_part = jnp.sin(angles)
    upper_rows = jnp.concatenate([cosine, -sine_part], axis=1)
    lower_rows = jnp.concatenate([sine_part, cosine], axis=1)
    return (jnp.concatenate([upper_rows, lower_rows], axis=0) / math.sqrt(CHANNELS)).astype(
        jnp.bfloat16
    )


def shards(voltages, beam_delay, bandpass, trial_delays):
    local_channels = voltages.shape[0]
    position = lax.axis_index("ch")
    channels = position * local_channels + jnp.arange(local_channels, dtype=jnp.int32)
    forward = forward_table()
    backward = inverse_table()
    beam_power = lax.map(
        functools.partial(channel_power, beam_delay), (channels, voltages, bandpass)
    )
    channel_mean = lax.psum(jnp.sum(beam_power, axis=0), "ch") / CHANNELS
    spectra = jnp.einsum(
        "cbt,tkf->kfcb", beam_power - channel_mean, forward, precision=lax.Precision.HIGHEST
    )
    spectra = spectra.astype(jnp.bfloat16)
    spectra_block = lax.all_to_all(spectra, "ch", split_axis=1, concat_axis=2, tiled=True)
    local_freqs = spectra_block.shape[1]

    def one_frequency(freq_index):
        freq_slice = lax.dynamic_index_in_dim(spectra_block, freq_index, 1, keepdims=False)
        phasors = phasor_block(trial_delays, position * local_freqs + freq_index + 1)
        product = jnp.dot(
            phasors,
            freq_slice.reshape(2 * freq_slice.shape[1], freq_slice.shape[2]),
            preferred_element_type=jnp.float32,
        )
        return product.astype(jnp.bfloat16).reshape(2, trial_delays.shape[0], freq_slice.shape[2])

    dedispersed_spectra = lax.map(one_frequency, jnp.arange(local_freqs, dtype=jnp.int32))
    series = jnp.einsum(
        "fkdb,fkt->dbt",
        lax.all_to_all(dedispersed_spectra, "ch", split_axis=2, concat_axis=0, tiled=True),
        backward,
        preferred_element_type=jnp.float32,
    )
    return series.astype(jnp.bfloat16)


def solution(mesh):
    return jax.shard_map(
        shards,
        mesh=mesh,
        in_specs=(P(("pt", "ch"), None, None, None), P("pt", None), P("ch"), P()),
        out_specs=P(("pt", "ch"), None, None),
        check_vma=False,
    )
```

profile of v0, /device:TPU:8, one launch (start us, length us, event | category | flops | bytes accessed | tf_op | source)
XLA Modules:
  0.0 1003.5 jit_solution(11758832814748078061)
XLA Ops:
  6.5 184.7 %while.24 = (s32[]{:T(128)}, f32[16,256,512]{1,2,0:T(8,128)}, s32[16]{0:T(128)S(1)}, s32[256,64]{0,1:T(8,128)}, bf16[16,2,64,2048]{3,2,1,0:T(8,128)(2,1)}, /*ind...) while((s32[]{:T(128)}, f32[16,256,512]{1,2,0:T(8,128)}, s32[16]{0:T(128)S(1)}, ...), condition=%wide.region_2.3_spmd, body=%wide.region_0.2_spmd.sunk | while | flops 271106048 | bytes 24577468 | solution.py:79
  12.9 1.9 reshape.244
  35.9 1.9 reshape.244
  47.5 1.9 reshape.244
  59.0 1.9 reshape.244
  70.6 1.9 reshape.244
  116.7 1.9 reshape.244
  191.3 4.8 reduce_sum.21
  196.1 2.1 fusion.55
  198.2 589.0 %all-reduce.2.cloned.1.call-done = f32[256,512]{0,1:T(8,128)} async-done(((f32[256,512]{0,1:T(8,128)}), f32[256,512]{0,1:T(8,128)}) %all-reduce.2.cloned.1.call-update) | async-done | bytes 524304 | tf_op jit(solution)/shard_map/psum | solution.py:82
  788.3 16.1 %fusion.29 = bf16[2,256,16,256]{3,1,2,0:T(8,128)(2,1)S(1)} fusion(f32[16,256,512]{1,2,0:T(8,128)} %get-tuple-element.165, f32[256,512]{0,1:T(8,128)S(1)} %broadcast_multiply_fusion, f32[512,1,256]{0,2,1:T(8,128)S(1)} %get-tuple-element.200, f32[512,1,256]{0,2,1:T(8,128)S(1)} %get-tuple-element.199), kind=kOutput, calls=%fused_computation.40 | convolution fusion | flops 12889620480 | bytes 14155776 | tf_op jit(solution)/shard_map/cbt,tkf->kfcb/dot_general | solution.py:83
  804.4 4.4 copy.16
  808.7 29.8 %all-to-all-start = ((bf16[2,256,16,256]{3,2,0,1:T(8,128)(2,1)}), bf16[2,256,16,256]{3,2,0,1:T(8,128)(2,1)}, u32[]{:S(2)}, u32[]{:S(2)}) async-start(bf16[2,256,16,256]{3,2,0,1:T(8,128)(2,1)} %copy.16), calls=%async_computation | async-start | bytes 8388608 | tf_op jit(solution)/shard_map/all_to_all | solution.py:87
  838.6 51.6 %all-to-all-done = bf16[2,256,16,256]{3,2,0,1:T(8,128)(2,1)} async-done(((bf16[2,256,16,256]{3,2,0,1:T(8,128)(2,1)}), bf16[2,256,16,256]{3,2,0,1:T(8,128)(2,1)}, u32[]{:S(2)}, u32[]{:S(2)}) %all-to-all-start) | async-done | bytes 4194336 | tf_op jit(solution)/shard_map/all_to_all | solution.py:87
  890.2 4.7 copy.17
  894.9 61.0 %while.25 = (s32[]{:T(128)}, bf16[4,2,512,256]{3,1,0,2:T(2,128)(2,1)}, s32[4]{0:T(128)S(1)}, s32[]{:T(128)}, s32[512,1024]{1,0:T(8,128)S(1)}, /*index=5*/bf16[2,...) while((s32[]{:T(128)}, bf16[4,2,512,256]{3,1,0,2:T(2,128)(2,1)}, s32[4]{0:T(128)S(1)}, s32[]{:T(128)}, ...), condition=%wide.region_6.7_spmd, body=%wide.region_5.6_spmd.sunk | while | flops 1092354048 | bytes 19399340 | solution.py:100
  899.3 8.3 fusion.82
  914.5 8.3 fusion.82
  929.8 8.3 fusion.82
  945.0 8.3 fusion.82
  956.0 7.2 all-to-all-start.1
  963.1 2.1 fusion.54
  965.3 27.6 %all-to-all-done.1 = bf16[4,2,512,256]{3,1,0,2:T(2,128)(2,1)S(1)} async-done(((bf16[4,2,512,256]{3,1,0,2:T(2,128)(2,1)}), bf16[4,2,512,256]{3,1,0,2:T(2,128)(2,1)S(1)}, u32[]{:S(2)}, u32[]{:S(2)}) %all-to-all-start.1) | async-done | bytes 2097184 | tf_op jit(solution)/shard_map/all_to_all | solution.py:103
  993.5 3.1 bitcast_convert_fusion
  (214 shorter events, 171.7 us)
Async XLA Ops:
  6.5 780.7 %all-reduce.2.cloned.1.call-start = ((), (), s32[]{:S(2)}) async-start(), calls=%async_computation.2 | async-start | bytes 1048576 | tf_op jit(solution)/shard_map/psum | solution.py:82
  14.7 1.3 copy-start.1
  26.3 1.3 copy-start.1
  37.8 1.3 copy-start.1
  49.4 1.3 copy-start.1
  60.9 1.3 copy-start.1
  72.4 1.3 copy-start.1
  84.0 1.3 copy-start.1
  95.5 1.3 copy-start.1
  107.1 1.3 copy-start.1
  118.6 1.3 copy-start.1
  130.1 1.3 copy-start.1
  141.7 1.3 copy-start.1
  153.2 1.3 copy-start.1
  164.8 1.3 copy-start.1
  176.3 1.3 copy-start.1
  187.9 1.3 copy-start.1
  808.7 81.5 %all-to-all-start = ((bf16[2,256,16,256]{3,2,0,1:T(8,128)(2,1)}), bf16[2,256,16,256]{3,2,0,1:T(8,128)(2,1)}, u32[]{:S(2)}, u32[]{:S(2)}) async-start(bf16[2,256,16,256]{3,2,0,1:T(8,128)(2,1)} %copy.16), calls=%async_computation | async-start | bytes 8388608 | tf_op jit(solution)/shard_map/all_to_all | solution.py:87
  890.2 4.7 copy-start
  956.0 36.9 %all-to-all-start.1 = ((bf16[4,2,512,256]{3,1,0,2:T(2,128)(2,1)}), bf16[4,2,512,256]{3,1,0,2:T(2,128)(2,1)S(1)}, u32[]{:S(2)}, u32[]{:S(2)}) async-start(bf16[4,2,512,256]{3,1,0,2:T(2,128)(2,1)} %get-tuple-element.166), calls=%async_computation.1 | async-start | bytes 4194304 | tf_op jit(solution)/shard_map/all_to_all | solution.py:103
Sparse Core Ops, SparseCore 0:
  196.2 590.9 all-reduce.1
where the time goes:
time: 1010 us; the launch traced here: 1000 us
  waiting for transfers between devices  668 us (66%)
  local copies, waits for them, and re-layouts  118 us (12%)
  other arithmetic  99.7 us (10%)
  starting transfers between devices  37 us (4%)
  matrix products  36 us (4%)
  loops' own time  31.5 us (3%)
  between operations  13.5 us (1%)
    psum x1, waiting for transfers between devices, shards(): channel_mean = lax.psum(jnp.sum(beam_power, axis=0), 'ch') / CHANNELS  589 us
    all_to_all x1, waiting for transfers between devices, shards(): lax.all_to_all(spectra, 'ch', split_axis=1, concat_axis=2, tiled=True)  51.6 us
    dynamic_slice x48, local copies, waits for them, and re-layouts, shards(): lax.map(functools.partial(channel_power, beam_delay), (channels, voltages...  36.1 us
    neg x4, other arithmetic, phasor_block(): upper_rows = jnp.concatenate([cosine, -sine_part], axis=1)  33.1 us
    all_to_all x1, starting transfers between devices, shards(): lax.all_to_all(spectra, 'ch', split_axis=1, concat_axis=2, tiled=True)  29.8 us
    reshape x16, local copies, waits for them, and re-layouts, channel_power(): squared.reshape(beam_count, squared.shape[1] // INTEG, INTEG)  29.8 us
    add x16, local copies, waits for them, and re-layouts, channel_power(): squared = beamformed[:beam_count] ** 2 + beamformed[beam_count:] ** 2  29 us
    all_to_all x1, waiting for transfers between devices, shards(): lax.all_to_all(dedispersed_spectra, 'ch', split_axis=2, concat_axis=0, ti...  27.6 us
  transfers between devices with their start and end apart: 3, of which 3 were waited for; matrix products, arithmetic and copies ran while one was open for 0% of the time, Pallas kernels for 0%

commit v1 on v0

v1 whole, which is shorter than its diff:
```python
import functools
import math

import numpy as np
import jax
import jax.numpy as jnp
from jax import lax
from jax.experimental import pallas as pl
from jax.experimental.pallas import tpu as pltpu
from jax.sharding import PartitionSpec as P

CHANNELS = 1024
ANTENNAS = 64
BEAMS = 256
NT = 512
INTEG = 4
TRIALS = 512
S_RAW = 2048
NF = 256
DEVICES = 64
LOCAL_CHANNELS = CHANNELS // DEVICES
LOCAL_TRIALS = TRIALS // DEVICES
LOCAL_FREQS = NF // DEVICES
PARTS_OF_F = 2 * LOCAL_FREQS
HALF = NT // 2
LANES = 128
PHASE_PERIOD = 4096
CHUNKS = 1

f32 = jnp.float32
bf16 = jnp.bfloat16


def _fit(function, terms, odd):
    nodes = np.cos(np.pi * (np.arange(400) + 0.5) / 400) * 0.5
    nodes = nodes[nodes > 0]
    squares = nodes * nodes
    target = function(np.pi * nodes)
    powers = np.stack([squares**k for k in range(terms)], axis=1)
    if odd:
        powers = powers * nodes[:, None]
    return [float(c) for c in np.linalg.lstsq(powers, target, rcond=None)[0]]


SIN_TERMS = _fit(np.sin, 6, True)
COS_TERMS = _fit(np.cos, 6, False)


def circle(turns, scale):
    part = turns - jnp.floor(turns + 0.5)
    square = part * part
    sine = jnp.full_like(square, SIN_TERMS[-1])
    for term in SIN_TERMS[-2::-1]:
        sine = sine * square + term
    sine = sine * part
    cosine = jnp.full_like(square, COS_TERMS[-1])
    for term in COS_TERMS[-2::-1]:
        cosine = cosine * square + term
    return scale - (2.0 * scale) * (sine * sine), (2.0 * scale) * (sine * cosine)


def split_halves(x):
    high = x.astype(bf16)
    return high, (x - high.astype(f32)).astype(bf16)


FINAL_STEPS = 8
contract_first = (((0,), (0,)), ((), ()))


def power_kernel(base_ref, gain_ref, delay_ref, v_ref, power_ref, sum_ref, squares_ref):
    step = pl.program_id(0)
    nb = delay_ref.shape[1]
    channel = (base_ref[0] + step + CHANNELS).astype(f32)
    turns = delay_ref[...].astype(f32) * (channel * (1.0 / PHASE_PERIOD))
    cosine, sine = circle(turns, 1.0 / math.sqrt(2 * ANTENNAS))
    upper = jnp.concatenate([cosine, -sine], axis=1)
    lower = jnp.concatenate([sine, cosine], axis=1)
    weights = jnp.concatenate([upper, lower], axis=0).astype(bf16)
    rows = 256
    for block in range(S_RAW // rows):
        beamformed = lax.dot_general(
            v_ref[0, :, block * rows : (block + 1) * rows], weights, contract_first, preferred_element_type=f32
        )
        squared = beamformed[:, :nb] ** 2 + beamformed[:, nb:] ** 2
        for g in range(nb // LANES):
            squares_ref[g, block * rows : (block + 1) * rows, :] = squared[:, g * LANES : (g + 1) * LANES]
    gain = gain_ref[step] * (1.0 / INTEG)
    for g in range(nb // LANES):
        lanes = slice(g * LANES, (g + 1) * LANES)
        ref = squares_ref.at[g]
        first, second = [
            sum(ref[pl.ds(start + j, HALF, stride=INTEG), :] for j in range(INTEG)) * gain
            for start in (0, HALF * INTEG)
        ]
        for parity, power in ((0, first - second), (1, first + second)):
            power_ref[0, parity, :, lanes] = power
            before = jnp.where(step == 0, 0.0, sum_ref[parity, :, lanes])
            sum_ref[parity, :, lanes] = before + power


def transform(high_ref, low_ref, parity, values):
    if parity == 1:
        values = values - jnp.mean(values, axis=0, keepdims=True)
    high, low = split_halves(values)
    spectra = jnp.dot(high_ref[parity], high, preferred_element_type=f32)
    spectra += jnp.dot(low_ref[parity], high, preferred_element_type=f32)
    return spectra + jnp.dot(high_ref[parity], low, preferred_element_type=f32)


def transform_kernel(power_ref, sum_ref, high_ref, low_ref, spectra_ref):
    step = pl.program_id(0)
    nb = sum_ref.shape[2]

    @pl.when(step == 0)
    def build_tables():
        for parity in range(2):
            row = lax.broadcasted_iota(jnp.int32, (HALF, HALF), 0)
            time = lax.broadcasted_iota(jnp.int32, (HALF, HALF), 1)
            freq = 8 * (row // 8) + 2 * ((row % 8) // 2) + 1 + parity
            turns = (freq.astype(f32) * time.astype(f32)) * (1.0 / NT)
            cosine, sine = circle(turns, 1.0 / math.sqrt(NT))
            high, low = split_halves(jnp.where(row % 2 == 0, cosine, -sine))
            high_ref[parity] = high
            low_ref[parity] = low

    for parity in range(2):
        values = power_ref[0, parity] - sum_ref[parity] * (1.0 / LOCAL_CHANNELS)
        spectra = transform(high_ref, low_ref, parity, values)
        for g in range(nb // LANES):
            spectra_ref.at[g][pl.ds(parity * HALF * LOCAL_CHANNELS + step, HALF, stride=LOCAL_CHANNELS), :] = (
                spectra[:, g * LANES : (g + 1) * LANES]
            )


def centre_kernel(sum_ref, mean_ref, high_ref, low_ref, spectra_ref, out_ref, shift_ref):
    step = pl.program_id(0)
    nb = sum_ref.shape[2]

    @pl.when(step == 0)
    def shifts():
        for parity in range(2):
            difference = sum_ref[parity] * (1.0 / LOCAL_CHANNELS) - mean_ref[parity]
            shift_ref[parity * HALF : (parity + 1) * HALF, :] = transform(high_ref, low_ref, parity, difference)

    dests = DEVICES // FINAL_STEPS
    rows = dests * PARTS_OF_F
    start = pl.multiple_of(step * rows, rows)
    for g in range(nb // LANES):
        lanes = slice(g * LANES, (g + 1) * LANES)
        shift = shift_ref[pl.ds(start, rows), lanes]
        for dest in range(dests):
            for j in range(PARTS_OF_F):
                row = dest * PARTS_OF_F + j
                values = spectra_ref[g, row * LOCAL_CHANNELS : (row + 1) * LOCAL_CHANNELS, :]
                out_ref[dest, j, :, lanes] = (values + shift[row : row + 1, :]).astype(bf16)


def phasor_kernel(base_ref, delays_ref, order_ref, cos_ref, sin_ref):
    delays = delays_ref[...].astype(f32)
    for j in range(LOCAL_FREQS):
        factor = (base_ref[0] + 2 * j).astype(f32) * (1.0 / NT)
        cosine, sine = circle(delays * factor, 1.0 / math.sqrt(CHANNELS))
        cos_ref[j] = cosine.astype(bf16)
        sin_ref[j] = sine.astype(bf16)


OUT_STEPS = 4


def dedisperse_kernel(values_ref, cos_ref, sin_ref, out_ref, acc_ref):
    step = pl.program_id(0)
    nb = values_ref.shape[3]
    groups = nb // LANES

    @pl.when(step < LOCAL_FREQS)
    def one_frequency():
        real_in = values_ref[:, 0].reshape(CHANNELS, nb)
        imaginary_in = values_ref[:, 1].reshape(CHANNELS, nb)
        dot = functools.partial(jnp.dot, preferred_element_type=f32)
        real = dot(cos_ref[0], real_in) - dot(sin_ref[0], imaginary_in)
        imaginary = dot(sin_ref[0], real_in) + dot(cos_ref[0], imaginary_in)
        for k, part in enumerate((real, imaginary)):
            for g in range(groups):
                acc_ref.at[g][pl.ds(2 * step + k, TRIALS, stride=PARTS_OF_F), :] = part[:, g * LANES : (g + 1) * LANES]

    @pl.when(step >= LOCAL_FREQS)
    def finish():
        dests = DEVICES // OUT_STEPS
        rows = dests * LOCAL_TRIALS * PARTS_OF_F
        start = pl.multiple_of((step - LOCAL_FREQS) * rows, rows)
        for g in range(groups):
            values = acc_ref[g, pl.ds(start, rows), :].reshape(dests, LOCAL_TRIALS, PARTS_OF_F, LANES)
            out_ref[:, :, :, g * LANES : (g + 1) * LANES] = values.astype(bf16)


def inverse_kernel(values_ref, table_ref, out_ref):
    nb = values_ref.shape[3]
    values = values_ref[:, 0].astype(f32).reshape(DEVICES * PARTS_OF_F, nb).astype(bf16)
    odd = lax.dot_general(values[:HALF], table_ref[0], contract_first, preferred_element_type=f32)
    even = lax.dot_general(values[HALF:], table_ref[1], contract_first, preferred_element_type=f32)
    out_ref[0, :, :HALF] = (even + odd).astype(bf16)
    out_ref[0, :, HALF:] = (even - odd).astype(bf16)


def inverse_into(values_ref, table_ref, filled_ref, out_ref):
    inverse_kernel(values_ref, table_ref, out_ref)


VMEM_LIMIT = 56 * 1024 * 1024
PARAMS = pltpu.CompilerParams(dimension_semantics=("arbitrary",), vmem_limit_bytes=VMEM_LIMIT)


def cost(flops, size):
    return pl.CostEstimate(flops=int(flops), bytes_accessed=int(size), transcendentals=0)


def whole(shape):
    return pl.BlockSpec(shape, lambda i: (0,) * len(shape))


def power_call(chunk, nb, base, bandpass, delays, voltages):
    smem = pl.BlockSpec(memory_space=pltpu.SMEM)
    return pl.pallas_call(
        power_kernel,
        grid=(LOCAL_CHANNELS,),
        in_specs=[
            smem,
            smem,
            pl.BlockSpec((ANTENNAS, nb), lambda i: (0, chunk)),
            pl.BlockSpec((1, 2 * ANTENNAS, S_RAW), lambda i: (i, 0, 0)),
        ],
        out_specs=[pl.BlockSpec((1, 2, HALF, nb), lambda i: (i, 0, 0, 0)), whole((2, HALF, nb))],
        out_shape=[
            jax.ShapeDtypeStruct((LOCAL_CHANNELS, 2, HALF, nb), f32),
            jax.ShapeDtypeStruct((2, HALF, nb), f32),
        ],
        scratch_shapes=[pltpu.VMEM((nb // LANES, S_RAW, LANES), f32)],
        compiler_params=PARAMS,
        cost_estimate=cost(9e9 * nb / BEAMS, 17e6),
        name="power",
    )(base, bandpass, delays, voltages)


def transform_call(nb, power, sums):
    groups = nb // LANES
    table = jax.ShapeDtypeStruct((2, HALF, HALF), bf16)
    return pl.pallas_call(
        transform_kernel,
        grid=(LOCAL_CHANNELS,),
        in_specs=[pl.BlockSpec((1, 2, HALF, nb), lambda i: (i, 0, 0, 0)), whole((2, HALF, nb))],
        out_specs=[
            whole((2, HALF, HALF)),
            whole((2, HALF, HALF)),
            whole((groups, NT * LOCAL_CHANNELS, LANES)),
        ],
        out_shape=[table, table, jax.ShapeDtypeStruct((groups, NT * LOCAL_CHANNELS, LANES), f32)],
        compiler_params=PARAMS,
        cost_estimate=cost(8e9 * nb / BEAMS, 17e6),
        name="transform",
    )(power, sums)


def centre_call(nb, sums, mean, high, low, spectra):
    groups = nb // LANES
    dests = DEVICES // FINAL_STEPS
    return pl.pallas_call(
        centre_kernel,
        grid=(FINAL_STEPS,),
        in_specs=[
            whole((2, HALF, nb)),
            whole((2, HALF, nb)),
            whole((2, HALF, HALF)),
            whole((2, HALF, HALF)),
            pl.BlockSpec((groups, dests * PARTS_OF_F * LOCAL_CHANNELS, LANES), lambda i: (0, i, 0)),
        ],
        out_specs=pl.BlockSpec((dests, PARTS_OF_F, LOCAL_CHANNELS, nb), lambda i: (i, 0, 0, 0)),
        out_shape=jax.ShapeDtypeStruct((DEVICES, PARTS_OF_F, LOCAL_CHANNELS, nb), bf16),
        scratch_shapes=[pltpu.VMEM((NT, nb), f32)],
        compiler_params=PARAMS,
        cost_estimate=cost(1e9 * nb / BEAMS, 13e6),
        name="centre",
    )(sums, mean, high, low, spectra)


def phasor_call(first_freq, trial_delays, order):
    rows = 32
    shape = jax.ShapeDtypeStruct((LOCAL_FREQS, TRIALS, CHANNELS), bf16)
    block = pl.BlockSpec((LOCAL_FREQS, rows, CHANNELS), lambda i: (0, i, 0))
    return pl.pallas_call(
        phasor_kernel,
        grid=(TRIALS // rows,),
        in_specs=[
            pl.BlockSpec(memory_space=pltpu.SMEM),
            pl.BlockSpec((rows, CHANNELS), lambda i: (i, 0)),
            pl.BlockSpec(memory_space=pl.ANY),
        ],
        out_specs=[block, block],
        out_shape=[shape, shape],
        compiler_params=PARAMS,
        cost_estimate=pl.CostEstimate(flops=8_000_000_000, bytes_accessed=10_000_000, transcendentals=0),
        name="phasors",
    )(first_freq, trial_delays, order)


def dedisperse_call(nb, received, cosines, sines):
    last = LOCAL_FREQS - 1
    dests = DEVICES // OUT_STEPS
    phasor_block = pl.BlockSpec((1, TRIALS, CHANNELS), lambda i: (jnp.minimum(i, last), 0, 0))
    return pl.pallas_call(
        dedisperse_kernel,
        grid=(LOCAL_FREQS + OUT_STEPS,),
        in_specs=[
            pl.BlockSpec((DEVICES, 2, LOCAL_CHANNELS, nb), lambda i: (0, jnp.minimum(i, last), 0, 0)),
            phasor_block,
            phasor_block,
        ],
        out_specs=pl.BlockSpec(
            (dests, LOCAL_TRIALS, PARTS_OF_F, nb), lambda i: (jnp.maximum(i - LOCAL_FREQS, 0), 0, 0, 0)
        ),
        out_shape=jax.ShapeDtypeStruct((DEVICES, LOCAL_TRIALS, PARTS_OF_F, nb), bf16),
        scratch_shapes=[pltpu.VMEM((nb // LANES, TRIALS * PARTS_OF_F, LANES), f32)],
        compiler_params=PARAMS,
        cost_estimate=cost(5e9 * nb / BEAMS, 15e6),
        name="dedisperse",
    )(received, cosines, sines)


def inverse_call(chunk, nb, received, table, filled):
    in_specs = [
        pl.BlockSpec((DEVICES, 1, LOCAL_TRIALS, nb), lambda i: (0, i, 0, 0)),
        pl.BlockSpec((2, HALF, HALF), lambda i: (0, 0, 0)),
    ]
    operands = [received, table]
    if filled is not None:
        in_specs.append(pl.BlockSpec(memory_space=pl.ANY))
        operands.append(filled)
    return pl.pallas_call(
        inverse_kernel if filled is None else inverse_into,
        grid=(LOCAL_TRIALS,),
        in_specs=in_specs,
        out_specs=pl.BlockSpec((1, nb, NT), lambda i: (i, chunk, 0)),
        out_shape=jax.ShapeDtypeStruct((LOCAL_TRIALS, BEAMS, NT), bf16),
        input_output_aliases={} if filled is None else {2: 0},
        compiler_params=PARAMS,
        cost_estimate=pl.CostEstimate(flops=1_000_000_000 * nb // BEAMS, bytes_accessed=4_000_000, transcendentals=0),
        name="inverse",
    )(*operands)


def shards(voltages, beam_delay, bandpass, trial_delays):
    position = lax.axis_index("ch").astype(jnp.int32)
    base = (position * LOCAL_CHANNELS).reshape(1)
    owners = DEVICES // 2
    first_freq = (8 * (position % owners) + 1 + position // owners).reshape(1)
    rows = voltages.reshape(LOCAL_CHANNELS, 2 * ANTENNAS, S_RAW)
    delays = beam_delay.T
    nb = BEAMS // CHUNKS
    exchange = functools.partial(lax.all_to_all, axis_name="ch", split_axis=0, concat_axis=0, tiled=True)
    powers = [power_call(chunk, nb, base, bandpass, delays, rows) for chunk in range(CHUNKS)]
    spectra, table = [], None
    for power, sums in powers:
        part = exchange(sums.reshape(DEVICES, PARTS_OF_F, nb))
        high, low, transformed = transform_call(nb, power, sums)
        part = jnp.sum(part, axis=0, keepdims=True) / CHANNELS
        mean = exchange(jnp.broadcast_to(part, (DEVICES, PARTS_OF_F, nb))).reshape(2, HALF, nb)
        spectra.append(exchange(centre_call(nb, sums, mean, high, low, transformed)))
        table = high
    cosines, sines = phasor_call(first_freq, trial_delays, table)
    trials = [exchange(dedisperse_call(nb, received, cosines, sines)) for received in spectra]
    result = None
    for chunk in range(CHUNKS):
        result = inverse_call(chunk, nb, trials[chunk], table, result)
    return result


def solution(mesh):
    return jax.shard_map(
        shards,
        mesh=mesh,
        in_specs=(P(("pt", "ch"), None, None, None), P("pt", None), P("ch"), P()),
        out_specs=P(("pt", "ch"), None, None),
        check_vma=False,
    )
```

time: 1010 us -> 265 us (0.26)
  the two profiles are of different devices: /device:TPU:8 before, /device:TPU:1 now
where the time goes in v1:
time: 265 us; the launch traced here: 262 us
  blocking collectives  86.2 us (33%)
  waiting for transfers between devices  79.1 us (30%)
  Pallas kernels  76.1 us (29%)
  starting transfers between devices  18.3 us (7%)
    all_to_all x1, waiting for transfers between devices, shards(): exchange(centre_call(nb, sums, mean, high, low, transformed))  79.1 us
    all_to_all x1, blocking collectives, shards(): exchange(dedisperse_call(nb, received, cosines, sines))  56.9 us
    all_to_all x1, blocking collectives, shards(): part = exchange(sums.reshape(DEVICES, PARTS_OF_F, nb))  29.4 us
    pallas_call x1, Pallas kernels, power_call(): pl.pallas_call(power_kernel, grid=(LOCAL_CHANNELS,), in_specs=[smem, smem...  18.6 us
    pallas_call x1, Pallas kernels, transform_call(): pl.pallas_call(transform_kernel, grid=(LOCAL_CHANNELS,), in_specs=[pl.Blo...  17.9 us
    pallas_call x1, Pallas kernels, phasor_call(): pl.pallas_call(phasor_kernel, grid=(TRIALS // rows,), in_specs=[pl.BlockS...  14.6 us
    all_to_all x1, starting transfers between devices, shards(): exchange(centre_call(nb, sums, mean, high, low, transformed))  10.9 us
    pallas_call x1, Pallas kernels, dedisperse_call(): pl.pallas_call(dedisperse_kernel, grid=(LOCAL_FREQS + OUT_STEPS,), in_spe...  9.77 us
  transfers between devices with their start and end apart: 2, of which 1 were waited for; matrix products, arithmetic and copies ran while one was open for 0% of the time, Pallas kernels for 12%

profile of v1, /device:TPU:1, one launch (start us, length us, event | category | flops | bytes accessed | tf_op | source)
XLA Modules:
  0.0 261.6 jit_solution(689964864277856915)
XLA Ops:
  0.0 18.6 %power.1 = (f32[16,2,256,256]{3,2,1,0:T(8,128)}, f32[2,256,256]{2,1,0:T(8,128)}) custom-call(s32[1]{0:T(128)} %bitcast.base_ref, f32[16]{0:T(128)} %gain_ref.1, s32[64,256]{1,0:T(8,128)} %bitcast.9, bf16[16,128,2048]{2,1,0:T(8,128)(2,1)} %bitcast.8), custom_call_target="tpu_custom_call" | custom-call | flops 8999999488 | bytes 17000000 | tf_op jit(solution)/shard_map/power/pallas_call | solution.py:224
  18.6 29.4 %all_to_all.20 = f32[64,8,256]{2,1,0:T(8,128)S(1)} all-to-all(f32[64,8,256]{2,1,0:T(8,128)} %bitcast.6), channel_id=1, replica_groups=mesh['pt'=4,'ch'=64] {'ch'}, dimensions={0} | all-to-all | bytes 1048576 | tf_op jit(solution)/shard_map/all_to_all | solution.py:363
  48.0 0.1 reduce_sum.9
  48.1 0.8 broadcast_in_dim.2
  48.9 7.4 %all-to-all-start.1 = ((f32[64,8,256]{2,1,0:T(8,128)}), f32[64,8,256]{2,1,0:T(8,128)S(1)}, u32[]{:S(2)}, u32[]{:S(2)}) async-start(f32[64,8,256]{2,1,0:T(8,128)} %broadcast_in_dim.2), calls=%async_computation.1 | async-start | bytes 1048576 | tf_op jit(solution)/shard_map/all_to_all | solution.py:366
  56.3 17.9 %transform.1 = (bf16[2,256,256]{2,1,0:T(8,128)(2,1)}, bf16[2,256,256]{2,1,0:T(8,128)(2,1)}, f32[2,8192,128]{2,1,0:T(8,128)}) custom-call(f32[16,2,256,256]{3,2,1,0:T(8,128)} %get-tuple-element.13.power_ref, f32[2,256,256]{2,1,0:T(8,128)} %get-tuple-element.12.sum_ref), custom_call_target="tpu_custom_call" | custom-call | flops 8000000000 | bytes 17000000 | tf_op jit(solution)/shard_map/transform/pallas_call | solution.py:248
  74.2 0.0 all-to-all-done.1
  74.2 0.0 copy-start
  74.2 0.8 copy-done
  75.0 8.5 %centre.1 = bf16[64,8,16,256]{3,2,1,0:T(8,128)(2,1)} custom-call(f32[2,256,256]{2,1,0:T(8,128)} %get-tuple-element.12.sum_ref, f32[2,256,256]{2,1,0:T(8,128)} %bitcast.7, bf16[2,256,256]{2,1,0:T(8,128)(2,1)} %get-tuple-element.14.high_ref.order_ref.table_ref, bf16[2,256,256]{2,1,0:T(8,128)(2,1)} %get-tuple-element.15.low_ref, ...), custom_call_target="tpu_custom_call" | custom-call | flops 1000000000 | bytes 13000000 | tf_op jit(solution)/shard_map/centre/pallas_call | solution.py:267
  83.6 10.9 %all-to-all-start.2 = ((bf16[64,8,16,256]{3,2,1,0:T(8,128)(2,1)}), bf16[64,8,16,256]{3,2,1,0:T(8,128)(2,1)}, u32[]{:S(2)}, u32[]{:S(2)}) async-start(bf16[64,8,16,256]{3,2,1,0:T(8,128)(2,1)} %centre.1), calls=%async_computation.2 | async-start | bytes 8388608 | tf_op jit(solution)/shard_map/all_to_all | solution.py:367
  94.5 14.6 %phasors.1 = (bf16[4,512,1024]{2,1,0:T(8,128)(2,1)}, bf16[4,512,1024]{2,1,0:T(8,128)(2,1)}) custom-call(s32[1]{0:T(128)} %bitcast.5.base_ref, s32[512,1024]{1,0:T(8,128)} %delays_ref.1, bf16[2,256,256]{2,1,0:T(8,128)(2,1)} %get-tuple-element.14.high_ref.order_ref.table_ref), custom_call_target="tpu_custom_call" | custom-call | flops 8000000000 | bytes 10000000 | tf_op jit(solution)/shard_map/phasors/pallas_call | solution.py:290
  109.2 79.1 %all-to-all-done.2.values_ref = bf16[64,8,16,256]{3,2,1,0:T(8,128)(2,1)} async-done(((bf16[64,8,16,256]{3,2,1,0:T(8,128)(2,1)}), bf16[64,8,16,256]{3,2,1,0:T(8,128)(2,1)}, u32[]{:S(2)}, u32[]{:S(2)}) %all-to-all-start.2) | async-done | bytes 4194336 | tf_op jit(solution)/shard_map/all_to_all | solution.py:367
  188.3 9.8 %dedisperse.1 = bf16[64,8,8,256]{3,2,1,0:T(8,128)(2,1)} custom-call(bf16[64,8,16,256]{3,2,1,0:T(8,128)(2,1)} %all-to-all-done.2.values_ref, bf16[4,512,1024]{2,1,0:T(8,128)(2,1)} %get-tuple-element.17.cos_ref, bf16[4,512,1024]{2,1,0:T(8,128)(2,1)} %get-tuple-element.18.sin_ref), custom_call_target="tpu_custom_call" | custom-call | flops 5000000000 | bytes 15000000 | tf_op jit(solution)/shard_map/dedisperse/pallas_call | solution.py:310
  198.1 56.9 %all_to_all.21.values_ref = bf16[64,8,8,256]{3,2,1,0:T(8,128)(2,1)} all-to-all(bf16[64,8,8,256]{3,2,1,0:T(8,128)(2,1)} %dedisperse.1), channel_id=1, replica_groups=mesh['pt'=4,'ch'=64] {'ch'}, dimensions={0} | all-to-all | bytes 4194304 | tf_op jit(solution)/shard_map/all_to_all | solution.py:370
  254.9 6.7 %inverse.1 = bf16[8,256,512]{2,1,0:T(8,128)(2,1)} custom-call(bf16[64,8,8,256]{3,2,1,0:T(8,128)(2,1)} %all_to_all.21.values_ref, bf16[2,256,256]{2,1,0:T(8,128)(2,1)} %get-tuple-element.14.high_ref.order_ref.table_ref), custom_call_target="tpu_custom_call" | custom-call | flops 1000000000 | bytes 4000000 | tf_op jit(solution)/shard_map/inverse/pallas_call | solution.py:338
  (1 shorter events, 0.0 us)
Async XLA Ops:
  48.9 25.3 %all-to-all-start.1 = ((f32[64,8,256]{2,1,0:T(8,128)}), f32[64,8,256]{2,1,0:T(8,128)S(1)}, u32[]{:S(2)}, u32[]{:S(2)}) async-start(f32[64,8,256]{2,1,0:T(8,128)} %broadcast_in_dim.2), calls=%async_computation.1 | async-start | bytes 1048576 | tf_op jit(solution)/shard_map/all_to_all | solution.py:366
  74.2 0.8 copy-start
  83.6 104.7 %all-to-all-start.2 = ((bf16[64,8,16,256]{3,2,1,0:T(8,128)(2,1)}), bf16[64,8,16,256]{3,2,1,0:T(8,128)(2,1)}, u32[]{:S(2)}, u32[]{:S(2)}) async-start(bf16[64,8,16,256]{3,2,1,0:T(8,128)(2,1)} %centre.1), calls=%async_computation.2 | async-start | bytes 8388608 | tf_op jit(solution)/shard_map/all_to_all | solution.py:367

commit v2 on v1

v2 whole, which is shorter than its diff:
```python
import functools
import math

import numpy as np
import jax
import jax.numpy as jnp
from jax import lax
from jax.experimental import pallas as pl
from jax.experimental.pallas import tpu as pltpu
from jax.sharding import PartitionSpec as P

CHANNELS = 1024
ANTENNAS = 64
BEAMS = 256
NT = 512
INTEG = 4
TRIALS = 512
S_RAW = 2048
NF = 256
DEVICES = 64
LOCAL_CHANNELS = CHANNELS // DEVICES
LOCAL_TRIALS = TRIALS // DEVICES
LOCAL_FREQS = NF // DEVICES
PARTS_OF_F = 2 * LOCAL_FREQS
HALF = NT // 2
LANES = 128
PHASE_PERIOD = 4096
CHUNKS = 1

f32 = jnp.float32
bf16 = jnp.bfloat16


def _fit(function, terms, odd):
    nodes = np.cos(np.pi * (np.arange(400) + 0.5) / 400) * 0.5
    nodes = nodes[nodes > 0]
    squares = nodes * nodes
    target = function(np.pi * nodes)
    powers = np.stack([squares**k for k in range(terms)], axis=1)
    if odd:
        powers = powers * nodes[:, None]
    return [float(c) for c in np.linalg.lstsq(powers, target, rcond=None)[0]]


SIN_TERMS = _fit(np.sin, 6, True)
COS_TERMS = _fit(np.cos, 6, False)


def circle(turns, scale):
    part = turns - jnp.floor(turns + 0.5)
    square = part * part
    sine = jnp.full_like(square, SIN_TERMS[-1])
    for term in SIN_TERMS[-2::-1]:
        sine = sine * square + term
    sine = sine * part
    cosine = jnp.full_like(square, COS_TERMS[-1])
    for term in COS_TERMS[-2::-1]:
        cosine = cosine * square + term
    return scale - (2.0 * scale) * (sine * sine), (2.0 * scale) * (sine * cosine)


def split_halves(x):
    high = x.astype(bf16)
    return high, (x - high.astype(f32)).astype(bf16)


FINAL_STEPS = 4
contract_first = (((0,), (0,)), ((), ()))


POWER_STEP = 4
TRANSFORM_STEP = 4


def power_kernel(base_ref, gain_ref, delay_ref, v_ref, order_ref, power_ref, sum_ref, squares_ref):
    step = pl.program_id(0)
    nb = delay_ref.shape[1]
    rows = 256

    @pl.when(step == 0)
    def clear():
        sum_ref[...] = jnp.zeros_like(sum_ref)

    for local in range(POWER_STEP):
        channel = step * POWER_STEP + local
        turns = delay_ref[...].astype(f32) * ((base_ref[0] + channel + CHANNELS).astype(f32) * (1.0 / PHASE_PERIOD))
        cosine, sine = circle(turns, 1.0 / math.sqrt(2 * ANTENNAS))
        upper = jnp.concatenate([cosine, -sine], axis=1)
        lower = jnp.concatenate([sine, cosine], axis=1)
        weights = jnp.concatenate([upper, lower], axis=0).astype(bf16)
        slot = local % 2
        for block in range(S_RAW // rows):
            beamformed = lax.dot_general(
                v_ref[local, :, block * rows : (block + 1) * rows], weights, contract_first, preferred_element_type=f32
            )
            squared = beamformed[:, :nb] ** 2 + beamformed[:, nb:] ** 2
            for g in range(nb // LANES):
                squares_ref[slot, g, block * rows : (block + 1) * rows, :] = squared[:, g * LANES : (g + 1) * LANES]
        gain = gain_ref[channel] * (1.0 / INTEG)
        for g in range(nb // LANES):
            lanes = slice(g * LANES, (g + 1) * LANES)
            ref = squares_ref.at[slot, g]
            first, second = [
                sum(ref[pl.ds(start + j, HALF, stride=INTEG), :] for j in range(INTEG)) * gain
                for start in (0, HALF * INTEG)
            ]
            for parity, power in ((0, first - second), (1, first + second)):
                power_ref[local, parity, :, lanes] = power
                sum_ref[parity, :, lanes] += power


def transform(table_ref, parity, values):
    if parity == 1:
        values = values - jnp.mean(values, axis=0, keepdims=True)
    high, low = split_halves(values)
    return jnp.dot(table_ref[parity], jnp.concatenate([high, high, low], axis=0), preferred_element_type=f32)


def transform_kernel(power_ref, sum_ref, table_ref, spectra_ref):
    step = pl.program_id(0)
    nb = sum_ref.shape[2]

    @pl.when(step == 0)
    def build_tables():
        for parity in range(2):
            row = lax.broadcasted_iota(jnp.int32, (HALF, HALF), 0)
            time = lax.broadcasted_iota(jnp.int32, (HALF, HALF), 1)
            freq = 8 * (row // 8) + 2 * ((row % 8) // 2) + 1 + parity
            turns = (freq.astype(f32) * time.astype(f32)) * (1.0 / NT)
            cosine, sine = circle(turns, 1.0 / math.sqrt(NT))
            high, low = split_halves(jnp.where(row % 2 == 0, cosine, -sine))
            table_ref[parity, :, :HALF] = high
            table_ref[parity, :, HALF : 2 * HALF] = low
            table_ref[parity, :, 2 * HALF :] = high

    for local in range(TRANSFORM_STEP):
        for parity in range(2):
            values = power_ref[local, parity] - sum_ref[parity] * (1.0 / LOCAL_CHANNELS)
            spectra = transform(table_ref, parity, values)
            start = parity * HALF * LOCAL_CHANNELS + step * TRANSFORM_STEP + local
            for g in range(nb // LANES):
                spectra_ref.at[g][pl.ds(start, HALF, stride=LOCAL_CHANNELS), :] = (
                    spectra[:, g * LANES : (g + 1) * LANES]
                )


def centre_kernel(sum_ref, mean_ref, table_ref, spectra_ref, out_ref, shift_ref):
    step = pl.program_id(0)
    nb = sum_ref.shape[2]

    @pl.when(step == 0)
    def shifts():
        for parity in range(2):
            difference = sum_ref[parity] * (1.0 / LOCAL_CHANNELS) - mean_ref[parity]
            shift_ref[parity * HALF : (parity + 1) * HALF, :] = transform(table_ref, parity, difference)

    dests = DEVICES // FINAL_STEPS
    rows = dests * PARTS_OF_F
    start = pl.multiple_of(step * rows, rows)
    for g in range(nb // LANES):
        lanes = slice(g * LANES, (g + 1) * LANES)
        shift = shift_ref[pl.ds(start, rows), lanes]
        for dest in range(dests):
            for j in range(PARTS_OF_F):
                row = dest * PARTS_OF_F + j
                values = spectra_ref[g, row * LOCAL_CHANNELS : (row + 1) * LOCAL_CHANNELS, :]
                out_ref[dest, j, :, lanes] = (values + shift[row : row + 1, :]).astype(bf16)


PHASOR_ROWS = 128
PHASOR_STEPS = TRIALS // PHASOR_ROWS


def phasor_kernel(plan_ref, delays_ref, *refs):
    cos_ref, sin_ref = refs[-2:]

    @pl.when(plan_ref[1] != 0)
    def make():
        delays = delays_ref[...].astype(f32)
        for j in range(LOCAL_FREQS):
            factor = (plan_ref[0] + 2 * j).astype(f32) * (1.0 / NT)
            cosine, sine = circle(delays * factor, 1.0 / math.sqrt(CHANNELS))
            cos_ref[j] = cosine.astype(bf16)
            sin_ref[j] = sine.astype(bf16)

    if len(refs) > 2:

        @pl.when((plan_ref[1] == 0) & (pl.program_id(0) == 0))
        def keep():
            cos_ref[...] = refs[0][...]
            sin_ref[...] = refs[1][...]


OUT_STEPS = 2


def dedisperse_kernel(values_ref, cos_ref, sin_ref, out_ref, acc_ref):
    step = pl.program_id(0)
    nb = values_ref.shape[3]
    groups = nb // LANES

    @pl.when(step < LOCAL_FREQS)
    def one_frequency():
        real_in = values_ref[:, 0].reshape(CHANNELS, nb)
        imaginary_in = values_ref[:, 1].reshape(CHANNELS, nb)
        dot = functools.partial(jnp.dot, preferred_element_type=f32)
        real = dot(cos_ref[0], real_in) - dot(sin_ref[0], imaginary_in)
        imaginary = dot(sin_ref[0], real_in) + dot(cos_ref[0], imaginary_in)
        for k, part in enumerate((real, imaginary)):
            for g in range(groups):
                acc_ref.at[g][pl.ds(2 * step + k, TRIALS, stride=PARTS_OF_F), :] = part[:, g * LANES : (g + 1) * LANES]

    @pl.when(step >= LOCAL_FREQS)
    def finish():
        dests = DEVICES // OUT_STEPS
        rows = dests * LOCAL_TRIALS * PARTS_OF_F
        start = pl.multiple_of((step - LOCAL_FREQS) * rows, rows)
        for g in range(groups):
            values = acc_ref[g, pl.ds(start, rows), :].reshape(dests, LOCAL_TRIALS, PARTS_OF_F, LANES)
            out_ref[:, :, :, g * LANES : (g + 1) * LANES] = values.astype(bf16)


INVERSE_STEP = 2


def inverse_kernel(values_ref, table_ref, out_ref):
    nb = values_ref.shape[3]
    for trial in range(INVERSE_STEP):
        values = values_ref[:, trial].astype(f32).reshape(DEVICES * PARTS_OF_F, nb).astype(bf16)
        odd = lax.dot_general(values[:HALF], table_ref[0], contract_first, preferred_element_type=f32)
        even = lax.dot_general(values[HALF:], table_ref[1], contract_first, preferred_element_type=f32)
        out_ref[trial, :, :HALF] = (even + odd).astype(bf16)
        out_ref[trial, :, HALF:] = (even - odd).astype(bf16)


def inverse_into(values_ref, table_ref, filled_ref, out_ref):
    inverse_kernel(values_ref, table_ref, out_ref)


VMEM_LIMIT = 56 * 1024 * 1024
PARAMS = pltpu.CompilerParams(dimension_semantics=("arbitrary",), vmem_limit_bytes=VMEM_LIMIT)


def cost(flops, size):
    return pl.CostEstimate(flops=int(flops), bytes_accessed=int(size), transcendentals=0)


def whole(shape):
    return pl.BlockSpec(shape, lambda i: (0,) * len(shape))


def power_call(chunk, nb, base, bandpass, delays, voltages, order):
    smem = pl.BlockSpec(memory_space=pltpu.SMEM)
    return pl.pallas_call(
        power_kernel,
        grid=(LOCAL_CHANNELS // POWER_STEP,),
        in_specs=[
            smem,
            smem,
            pl.BlockSpec((ANTENNAS, nb), lambda i: (0, chunk)),
            pl.BlockSpec((POWER_STEP, 2 * ANTENNAS, S_RAW), lambda i: (i, 0, 0)),
            pl.BlockSpec(memory_space=pl.ANY),
        ],
        out_specs=[pl.BlockSpec((POWER_STEP, 2, HALF, nb), lambda i: (i, 0, 0, 0)), whole((2, HALF, nb))],
        out_shape=[
            jax.ShapeDtypeStruct((LOCAL_CHANNELS, 2, HALF, nb), f32),
            jax.ShapeDtypeStruct((2, HALF, nb), f32),
        ],
        scratch_shapes=[pltpu.VMEM((2, nb // LANES, S_RAW, LANES), f32)],
        compiler_params=PARAMS,
        cost_estimate=cost(9e9 * nb / BEAMS, 17e6),
        name="power",
    )(base, bandpass, delays, voltages, order)


def transform_call(nb, power, sums):
    groups = nb // LANES
    table = jax.ShapeDtypeStruct((2, HALF, 3 * HALF), bf16)
    return pl.pallas_call(
        transform_kernel,
        grid=(LOCAL_CHANNELS // TRANSFORM_STEP,),
        in_specs=[pl.BlockSpec((TRANSFORM_STEP, 2, HALF, nb), lambda i: (i, 0, 0, 0)), whole((2, HALF, nb))],
        out_specs=[
            whole((2, HALF, 3 * HALF)),
            whole((groups, NT * LOCAL_CHANNELS, LANES)),
        ],
        out_shape=[table, jax.ShapeDtypeStruct((groups, NT * LOCAL_CHANNELS, LANES), f32)],
        compiler_params=PARAMS,
        cost_estimate=cost(8e9 * nb / BEAMS, 17e6),
        name="transform",
    )(power, sums)


def centre_call(nb, sums, mean, table, spectra):
    groups = nb // LANES
    dests = DEVICES // FINAL_STEPS
    return pl.pallas_call(
        centre_kernel,
        grid=(FINAL_STEPS,),
        in_specs=[
            whole((2, HALF, nb)),
            whole((2, HALF, nb)),
            whole((2, HALF, 3 * HALF)),
            pl.BlockSpec((groups, dests * PARTS_OF_F * LOCAL_CHANNELS, LANES), lambda i: (0, i, 0)),
        ],
        out_specs=pl.BlockSpec((dests, PARTS_OF_F, LOCAL_CHANNELS, nb), lambda i: (i, 0, 0, 0)),
        out_shape=jax.ShapeDtypeStruct((DEVICES, PARTS_OF_F, LOCAL_CHANNELS, nb), bf16),
        scratch_shapes=[pltpu.VMEM((NT, nb), f32)],
        compiler_params=PARAMS,
        cost_estimate=cost(1e9 * nb / BEAMS, 13e6),
        name="centre",
    )(sums, mean, table, spectra)


def phasor_call(active, first_freq, trial_delays, earlier=(), order=None):
    shape = jax.ShapeDtypeStruct((LOCAL_FREQS, TRIALS, CHANNELS), bf16)
    block = pl.BlockSpec((LOCAL_FREQS, PHASOR_ROWS, CHANNELS), lambda i, plan: (0, i * plan[1], 0))
    first = pl.BlockSpec((LOCAL_FREQS, PHASOR_ROWS, CHANNELS), lambda i, plan: (0, 0, 0))
    operands = [trial_delays, *earlier] + ([] if order is None else [order])
    in_specs = [pl.BlockSpec((PHASOR_ROWS, CHANNELS), lambda i, plan: (i * plan[1], 0))]
    in_specs += [first] * len(earlier) + [pl.BlockSpec(memory_space=pl.ANY)] * (order is not None)
    return pl.pallas_call(
        phasor_kernel,
        grid_spec=pltpu.PrefetchScalarGridSpec(
            num_scalar_prefetch=1, grid=(PHASOR_STEPS,), in_specs=in_specs, out_specs=[block, block]
        ),
        out_shape=[shape, shape],
        input_output_aliases={2: 0, 3: 1} if earlier else {},
        compiler_params=PARAMS,
        cost_estimate=cost(8e9, 10e6),
        name="phasors",
    )(jnp.stack([first_freq, active]), *operands)


def dedisperse_call(nb, received, cosines, sines):
    last = LOCAL_FREQS - 1
    dests = DEVICES // OUT_STEPS
    phasor_block = pl.BlockSpec((1, TRIALS, CHANNELS), lambda i: (jnp.minimum(i, last), 0, 0))
    return pl.pallas_call(
        dedisperse_kernel,
        grid=(LOCAL_FREQS + OUT_STEPS,),
        in_specs=[
            pl.BlockSpec((DEVICES, 2, LOCAL_CHANNELS, nb), lambda i: (0, jnp.minimum(i, last), 0, 0)),
            phasor_block,
            phasor_block,
        ],
        out_specs=pl.BlockSpec(
            (dests, LOCAL_TRIALS, PARTS_OF_F, nb), lambda i: (jnp.maximum(i - LOCAL_FREQS, 0), 0, 0, 0)
        ),
        out_shape=jax.ShapeDtypeStruct((DEVICES, LOCAL_TRIALS, PARTS_OF_F, nb), bf16),
        scratch_shapes=[pltpu.VMEM((nb // LANES, TRIALS * PARTS_OF_F, LANES), f32)],
        compiler_params=PARAMS,
        cost_estimate=cost(5e9 * nb / BEAMS, 15e6),
        name="dedisperse",
    )(received, cosines, sines)


def inverse_call(chunk, nb, received, table, filled):
    in_specs = [
        pl.BlockSpec((DEVICES, INVERSE_STEP, LOCAL_TRIALS, nb), lambda i: (0, i, 0, 0)),
        pl.BlockSpec((2, HALF, HALF), lambda i: (0, 0, 0)),
    ]
    operands = [received, table]
    if filled is not None:
        in_specs.append(pl.BlockSpec(memory_space=pl.ANY))
        operands.append(filled)
    return pl.pallas_call(
        inverse_kernel if filled is None else inverse_into,
        grid=(LOCAL_TRIALS // INVERSE_STEP,),
        in_specs=in_specs,
        out_specs=pl.BlockSpec((INVERSE_STEP, nb, NT), lambda i: (i, chunk, 0)),
        out_shape=jax.ShapeDtypeStruct((LOCAL_TRIALS, BEAMS, NT), bf16),
        input_output_aliases={} if filled is None else {2: 0},
        compiler_params=PARAMS,
        cost_estimate=pl.CostEstimate(flops=1_000_000_000 * nb // BEAMS, bytes_accessed=4_000_000, transcendentals=0),
        name="inverse",
    )(*operands)


def shards(voltages, beam_delay, bandpass, trial_delays):
    position = lax.axis_index("ch").astype(jnp.int32)
    base = (position * LOCAL_CHANNELS).reshape(1)
    owners = DEVICES // 2
    first_freq = 8 * (position % owners) + 1 + position // owners
    rows = voltages.reshape(LOCAL_CHANNELS, 2 * ANTENNAS, S_RAW)
    delays = beam_delay.T
    nb = BEAMS // CHUNKS
    exchange = functools.partial(lax.all_to_all, axis_name="ch", split_axis=0, concat_axis=0, tiled=True)
    early = lax.axis_index("pt").astype(jnp.int32) % 2
    phasors = phasor_call(early, first_freq, trial_delays)
    powers = [power_call(chunk, nb, base, bandpass, delays, rows, phasors[0]) for chunk in range(CHUNKS)]
    spectra = []
    for power, sums in powers:
        part = exchange(sums.reshape(DEVICES, PARTS_OF_F, nb))
        table, transformed = transform_call(nb, power, sums)
        part = jnp.sum(part, axis=0, keepdims=True) / CHANNELS
        mean = exchange(jnp.broadcast_to(part, (DEVICES, PARTS_OF_F, nb))).reshape(2, HALF, nb)
        sent = centre_call(nb, sums, mean, table, transformed)
        spectra.append(exchange(sent))
    cosines, sines = phasor_call(1 - early, first_freq, trial_delays, phasors, sent)
    trials = [exchange(dedisperse_call(nb, received, cosines, sines)) for received in spectra]
    result = None
    for chunk in range(CHUNKS):
        result = inverse_call(chunk, nb, trials[chunk], table, result)
    return result


def solution(mesh):
    return jax.shard_map(
        shards,
        mesh=mesh,
        in_specs=(P(("pt", "ch"), None, None, None), P("pt", None), P("ch"), P()),
        out_specs=P(("pt", "ch"), None, None),
        check_vma=False,
    )
```

time: 265 us -> 252 us (0.951)
  Pallas kernels: 76.1 us -> 63.3 us
  waiting for transfers between devices: 79.1 us -> 85.8 us
  blocking collectives: 86.2 us -> 82.3 us
    pallas_call x3 -> x4, Pallas kernels: 51.1 us -> 42.5 us  [the longest x2 16 us: phasor_call(): pl.pallas_call(phasor_kernel, grid_spec=pltpu.PrefetchScalarGridSpec(num_...]
    all_to_all x1, waiting for transfers between devices: 79.1 us -> 85.7 us  [shards(): spectra.append(exchange(sent))]
    all_to_all x1, blocking collectives: 29.4 us -> 26 us  [shards(): part = exchange(sums.reshape(DEVICES, PARTS_OF_F, nb))]
  transfers between devices with their start and end apart: 2 -> 2, of which waited for: 1 -> 2; matrix products, arithmetic and copies ran while one was open for 0% -> 0% of each run, Pallas kernels for 12% -> 7%
where the time goes in v2:
time: 252 us; the launch traced here: 251 us
  waiting for transfers between devices  85.8 us (34%)
  blocking collectives  82.3 us (33%)
  Pallas kernels  63.3 us (25%)
  starting transfers between devices  16.7 us (7%)
    all_to_all x1, waiting for transfers between devices, shards(): spectra.append(exchange(sent))  85.7 us
    all_to_all x1, blocking collectives, shards(): exchange(dedisperse_call(nb, received, cosines, sines))  56.3 us
    all_to_all x1, blocking collectives, shards(): part = exchange(sums.reshape(DEVICES, PARTS_OF_F, nb))  26 us
    pallas_call x2, Pallas kernels, phasor_call(): pl.pallas_call(phasor_kernel, grid_spec=pltpu.PrefetchScalarGridSpec(num_...  16 us
    pallas_call x1, Pallas kernels, power_call(): pl.pallas_call(power_kernel, grid=(LOCAL_CHANNELS // POWER_STEP,), in_spe...  13.8 us
    pallas_call x1, Pallas kernels, transform_call(): pl.pallas_call(transform_kernel, grid=(LOCAL_CHANNELS // TRANSFORM_STEP,)...  12.6 us
    all_to_all x1, starting transfers between devices, shards(): spectra.append(exchange(sent))  11.1 us
    pallas_call x1, Pallas kernels, dedisperse_call(): pl.pallas_call(dedisperse_kernel, grid=(LOCAL_FREQS + OUT_STEPS,), in_spe...  9.33 us
  transfers between devices with their start and end apart: 2, of which 2 were waited for; matrix products, arithmetic and copies ran while one was open for 0% of the time, Pallas kernels for 7%

profile of v2, /device:TPU:1, one launch (start us, length us, event | category | flops | bytes accessed | tf_op | source)
XLA Modules:
  0.0 251.0 jit_solution(1830985921681342045)
XLA Ops:
  0.0 0.6 pad_add_fusion.plan_ref
  0.6 12.0 %phasors.2 = (bf16[4,512,1024]{2,1,0:T(8,128)(2,1)}, bf16[4,512,1024]{2,1,0:T(8,128)(2,1)}) custom-call(s32[2]{0:T(128)} %pad_add_fusion.plan_ref, s32[512,1024]{1,0:T(8,128)} %delays_ref.3), custom_call_target="tpu_custom_call" | custom-call | flops 8000000000 | bytes 10000000 | tf_op jit(solution)/shard_map/phasors/pallas_call | solution.py:322
  12.5 13.8 %power.1 = (f32[16,2,256,256]{3,2,1,0:T(8,128)}, f32[2,256,256]{2,1,0:T(8,128)}) custom-call(s32[1]{0:T(128)} %bitcast.base_ref, f32[16]{0:T(128)} %gain_ref.1, s32[64,256]{1,0:T(8,128)} %bitcast.11, bf16[16,128,2048]{2,1,0:T(8,128)(2,1)} %bitcast.10, bf16[4,512,1024]{2,1,0:T(8,128)(2,1)} %get-tuple-element.13.order_ref.refs_0_), custom_call_target="tpu_custom_call" | custom-call | flops 8999999488 | bytes 17000000 | tf_op jit(solution)/shard_map/power/pallas_call | solution.py:254
  26.3 26.0 %all_to_all.20 = f32[64,8,256]{2,1,0:T(8,128)S(1)} all-to-all(f32[64,8,256]{2,1,0:T(8,128)} %bitcast.8), channel_id=1, replica_groups=mesh['pt'=4,'ch'=64] {'ch'}, dimensions={0} | all-to-all | bytes 1048576 | tf_op jit(solution)/shard_map/all_to_all | solution.py:394
  52.3 0.1 reduce_sum.9
  52.4 0.8 broadcast_in_dim.2
  53.2 5.6 %all-to-all-start.1 = ((f32[64,8,256]{2,1,0:T(8,128)}), f32[64,8,256]{2,1,0:T(8,128)S(1)}, u32[]{:S(2)}, u32[]{:S(2)}) async-start(f32[64,8,256]{2,1,0:T(8,128)} %broadcast_in_dim.2), calls=%async_computation.1 | async-start | bytes 1048576 | tf_op jit(solution)/shard_map/all_to_all | solution.py:397
  58.9 12.6 %transform.1 = (bf16[2,256,768]{2,1,0:T(8,128)(2,1)}, f32[2,8192,128]{2,1,0:T(8,128)}) custom-call(f32[16,2,256,256]{3,2,1,0:T(8,128)} %get-tuple-element.15.power_ref, f32[2,256,256]{2,1,0:T(8,128)} %get-tuple-element.14.sum_ref), custom_call_target="tpu_custom_call" | custom-call | flops 8000000000 | bytes 17000000 | tf_op jit(solution)/shard_map/transform/pallas_call | solution.py:279
  71.5 0.1 all-to-all-done.1
  71.6 0.0 copy-start
  71.6 0.8 copy-done
  72.4 7.0 %centre.1.refs_2_ = bf16[64,8,16,256]{3,2,1,0:T(8,128)(2,1)} custom-call(f32[2,256,256]{2,1,0:T(8,128)} %get-tuple-element.14.sum_ref, f32[2,256,256]{2,1,0:T(8,128)} %bitcast.9, bf16[2,256,768]{2,1,0:T(8,128)(2,1)} %get-tuple-element.16.table_ref, f32[2,8192,128]{2,1,0:T(8,128)} %get-tuple-element.17.spectra_ref), custom_call_target="tpu_custom_call" | custom-call | flops 1000000000 | bytes 13000000 | tf_op jit(solution)/shard_map/centre/pallas_call | solution.py:297
  79.3 11.1 %all-to-all-start.2 = ((bf16[64,8,16,256]{3,2,1,0:T(8,128)(2,1)}), bf16[64,8,16,256]{3,2,1,0:T(8,128)(2,1)}, u32[]{:S(2)}, u32[]{:S(2)}) async-start(bf16[64,8,16,256]{3,2,1,0:T(8,128)(2,1)} %centre.1.refs_2_), calls=%async_computation.2 | async-start | bytes 8388608 | tf_op jit(solution)/shard_map/all_to_all | solution.py:399
  90.4 0.7 pad_add_fusion.1.plan_ref
  91.1 4.1 %phasors.3 = (bf16[4,512,1024]{2,1,0:T(8,128)(2,1)}, bf16[4,512,1024]{2,1,0:T(8,128)(2,1)}) custom-call(s32[2]{0:T(128)} %pad_add_fusion.1.plan_ref, s32[512,1024]{1,0:T(8,128)} %delays_ref.3, bf16[4,512,1024]{2,1,0:T(8,128)(2,1)} %get-tuple-element.13.order_ref.refs_0_, ...), custom_call_target="tpu_custom_call", output_to_operand_aliasing={{0}: (2, {}), {1}: (3, {})} | custom-call | flops 8000000000 | bytes 10000000 | tf_op jit(solution)/shard_map/phasors/pallas_call | solution.py:322
  95.2 85.7 %all-to-all-done.2.values_ref = bf16[64,8,16,256]{3,2,1,0:T(8,128)(2,1)} async-done(((bf16[64,8,16,256]{3,2,1,0:T(8,128)(2,1)}), bf16[64,8,16,256]{3,2,1,0:T(8,128)(2,1)}, u32[]{:S(2)}, u32[]{:S(2)}) %all-to-all-start.2) | async-done | bytes 4194336 | tf_op jit(solution)/shard_map/all_to_all | solution.py:399
  180.9 9.3 %dedisperse.1 = bf16[64,8,8,256]{3,2,1,0:T(8,128)(2,1)} custom-call(bf16[64,8,16,256]{3,2,1,0:T(8,128)(2,1)} %all-to-all-done.2.values_ref, bf16[4,512,1024]{2,1,0:T(8,128)(2,1)} %get-tuple-element.19.cos_ref, bf16[4,512,1024]{2,1,0:T(8,128)(2,1)} %get-tuple-element.20.sin_ref), custom_call_target="tpu_custom_call" | custom-call | flops 5000000000 | bytes 15000000 | tf_op jit(solution)/shard_map/dedisperse/pallas_call | solution.py:339
  190.2 56.3 %all_to_all.21.values_ref = bf16[64,8,8,256]{3,2,1,0:T(8,128)(2,1)} all-to-all(bf16[64,8,8,256]{3,2,1,0:T(8,128)(2,1)} %dedisperse.1), channel_id=1, replica_groups=mesh['pt'=4,'ch'=64] {'ch'}, dimensions={0} | all-to-all | bytes 4194304 | tf_op jit(solution)/shard_map/all_to_all | solution.py:401
  246.5 4.5 %inverse.1 = bf16[8,256,512]{2,1,0:T(8,128)(2,1)} custom-call(bf16[64,8,8,256]{3,2,1,0:T(8,128)(2,1)} %all_to_all.21.values_ref, bf16[2,256,768]{2,1,0:T(8,128)(2,1)} %get-tuple-element.16.table_ref), custom_call_target="tpu_custom_call" | custom-call | flops 1000000000 | bytes 4000000 | tf_op jit(solution)/shard_map/inverse/pallas_call | solution.py:367
  (1 shorter events, 0.0 us)
Async XLA Ops:
  53.2 18.3 %all-to-all-start.1 = ((f32[64,8,256]{2,1,0:T(8,128)}), f32[64,8,256]{2,1,0:T(8,128)S(1)}, u32[]{:S(2)}, u32[]{:S(2)}) async-start(f32[64,8,256]{2,1,0:T(8,128)} %broadcast_in_dim.2), calls=%async_computation.1 | async-start | bytes 1048576 | tf_op jit(solution)/shard_map/all_to_all | solution.py:397
  71.6 0.8 copy-start
  79.3 101.5 %all-to-all-start.2 = ((bf16[64,8,16,256]{3,2,1,0:T(8,128)(2,1)}), bf16[64,8,16,256]{3,2,1,0:T(8,128)(2,1)}, u32[]{:S(2)}, u32[]{:S(2)}) async-start(bf16[64,8,16,256]{3,2,1,0:T(8,128)(2,1)} %centre.1.refs_2_), calls=%async_computation.2 | async-start | bytes 8388608 | tf_op jit(solution)/shard_map/all_to_all | solution.py:399
